TPU v7x, 32 devices: a whole 2x2x4 slice. The times are simulated.
32 devices in a mesh: sec: 4 (over y, x), dom: 8 (over z, core).
Axes of the slice: x: 2, y: 2, z: 4, core: 2. Of those that a mesh axis runs over, the one named last changes fastest.
Arguments:
- disp_coarse: float32 [4096], P('dom'), may hold values from -6 to 6
- support_ids: int32 [4, 8, 4], P('sec', 'dom'), may hold values from 0 to 7, all different within a row
- rbf_weights: bfloat16 [4, 8, 4, 512, 64], P('sec', 'dom'), may hold values from -0.125 to 0.125
- flow: float32 [4, 4, 512, 256], P('sec', None, 'dom'), may hold values from -6 to 6
- pivots: int32 [4096], replicated, may hold values from 0 to 4095, each once
- lower_inverse: float32 [4096, 4096], P('dom'), as said below
- upper_inverse: float32 [4096, 4096], P('dom'), as said below
Outputs:
- new_flow: float32 [4, 4, 512, 256], P('sec', None, 'dom')
- new_disp: float32 [4096], P('dom')
Inputs may be any that keep to these rules, and one draw needn't show every extreme that they name: `support_ids`: each row names 4 different structure blocks; every block is named by some row. `pivots`: each index once. `lower_inverse`: unit lower triangular. `upper_inverse`: upper triangular with a positive diagonal.
All inputs are finite; a program needn't handle non-finite values.
Results may differ from a plain program's by a relative error of at most 0.00035.
Values may be sent and summed in bfloat16 or wider, within the bound.
No kernel may reach another device: no remote copies, remote signals or barrier semaphores. Data moves between devices by JAX's collectives and lax.ppermute only.
A program may use at most 64 MiB of HBM per device.

v0:
```python
import functools

import jax
import jax.numpy as jnp
from jax import lax
from jax.experimental import pallas as pl
from jax.experimental.pallas import tpu as pltpu
from jax.sharding import PartitionSpec as P


ITERS = 4
REACH = 2


COURANT = 0.4
MACH = 0.5
DISSIPATION = 0.03125
FACE_AREA = 0.125

LANES = 128
SUB = 8
GROUP = LANES // 4


def padded_2(cells, sides, width):
    for axis, dim in sides:
        count = lax.axis_size(axis)
        head = lax.slice_in_dim(cells, 0, width, axis=dim)
        tail = lax.slice_in_dim(cells, cells.shape[dim] - width, cells.shape[dim], axis=dim)
        cells = jnp.concatenate(
            [
                lax.ppermute(tail, axis, [(i, (i + 1) % count) for i in range(count)]),
                cells,
                lax.ppermute(head, axis, [((i + 1) % count, i) for i in range(count)]),
            ],
            axis=dim,
        )
    return cells


def stencil(padded):
    z_extent = padded.shape[1]
    y_extent = padded.shape[2]
    y_padded = jnp.pad(padded, ((0, 0), (0, 0), (2, 2)))

    def zshift(offset):
        return y_padded[:, 2 + offset : z_extent - 2 + offset, 2 : y_extent + 2]

    def yshift(offset):
        return y_padded[:, 2 : z_extent - 2, 2 + offset : y_extent + 2 + offset]

    centre = zshift(0)
    z_slope = 0.5 * (zshift(1) - zshift(-1))
    y_slope = 0.5 * (yshift(1) - yshift(-1))
    z_fourth = zshift(2) - 4.0 * zshift(1) + 6.0 * centre - 4.0 * zshift(-1) + zshift(-2)
    y_fourth = yshift(2) - 4.0 * yshift(1) + 6.0 * centre - 4.0 * yshift(-1) + yshift(-2)
    damping = DISSIPATION * (z_fourth + y_fourth)
    density = centre[0] - COURANT * (MACH * z_slope[0] + z_slope[2] + y_slope[3]) - damping[0]
    pressure = centre[1] - COURANT * (MACH * z_slope[1] + z_slope[2] + y_slope[3]) - damping[1]
    along = centre[2] - COURANT * (MACH * z_slope[2] + z_slope[1]) - damping[2]
    normal = centre[3] - COURANT * (MACH * z_slope[3] + y_slope[1]) - damping[3]
    return jnp.stack([density, pressure, along, normal])


def with_rims(fields):
    return padded_2(fields, (("dom", 1),), 2)


def shards(disp_coarse, support_ids, rbf_weights, flow, pivots, lower_inverse, upper_inverse):
    block_size = disp_coarse.shape[0]
    domains = lax.axis_size("dom")
    coarse_table = lax.all_gather(
        disp_coarse.astype(jnp.bfloat16), "dom", axis=0, tiled=True
    ).reshape(domains, block_size)
    support = support_ids[0, 0]
    weights = rbf_weights[0, 0]
    matches = support[:, None] == lax.broadcasted_iota(jnp.int32, (support.shape[0], domains), 1)
    choose = matches.astype(jnp.bfloat16)
    picked = jnp.dot(choose, coarse_table, preferred_element_type=jnp.float32).astype(jnp.bfloat16)
    wall_motion = jnp.einsum("kj,kjz->z", picked, weights, preferred_element_type=jnp.float32)
    fields = flow[0].at[3, :, 0].set(wall_motion)
    for _ in range(ITERS):
        fields = stencil(with_rims(fields))
    push = (FACE_AREA * fields[1, :, 0]).astype(jnp.bfloat16)
    terms = jnp.einsum("kjz,z->kj", weights, push, preferred_element_type=jnp.float32)
    dense = jnp.einsum(
        "kb,kj->bj", matches.astype(jnp.float32), terms, precision=lax.Precision.HIGHEST
    )
    owned = lax.psum_scatter(dense, "dom", scatter_dimension=0, tiled=True)
    owned = lax.psum(owned, "sec")
    forces = lax.all_gather(owned, "dom", axis=0, tiled=True).reshape(-1)
    permuted = jnp.take(forces, pivots, axis=0)
    lower_part = jnp.dot(lower_inverse, permuted, precision=lax.Precision.HIGHEST)
    middle = lax.all_gather(lower_part, "dom", axis=0, tiled=True)
    solved = jnp.dot(upper_inverse, middle, precision=lax.Precision.HIGHEST)
    new_disp = 0.5 * disp_coarse + 0.5 * solved
    return (fields[None], new_disp)


def lane_index(shape):
    return lax.broadcasted_iota(jnp.int32, shape, 1)


def sweep(load, comps):
    shape = load(0, 0).shape
    lane = lane_index(shape)
    width = shape[1]

    def down(f, n):
        return jnp.where(lane >= n, pltpu.roll(f, n, 1), 0.0)

    def up(f, n):
        return jnp.where(lane < width - n, pltpu.roll(f, width - n, 1), 0.0)

    centre = [load(c, 0) for c in range(4)]
    need_y = set(comps) | ({3} if 0 in comps or 1 in comps else set()) | ({1} if 3 in comps else set())
    y_plus = {c: up(centre[c], 1) for c in need_y}
    y_minus = {c: down(centre[c], 1) for c in need_y}
    z_plus = [load(c, 1) for c in range(4)]
    z_minus = [load(c, -1) for c in range(4)]

    def z_slope(c):
        return 0.5 * (z_plus[c] - z_minus[c])

    def y_slope(c):
        return 0.5 * (y_plus[c] - y_minus[c])

    def damping(c):
        near = z_plus[c] + z_minus[c] + y_plus[c] + y_minus[c]
        far = load(c, 2) + load(c, -2) + up(centre[c], 2) + down(centre[c], 2)
        return DISSIPATION * (far - 4.0 * near + 12.0 * centre[c])

    out = {}
    if 0 in comps or 1 in comps:
        spread = z_slope(2) + y_slope(3)
    if 0 in comps:
        out[0] = centre[0] - COURANT * (MACH * z_slope(0) + spread) - damping(0)
    if 1 in comps:
        out[1] = centre[1] - COURANT * (MACH * z_slope(1) + spread) - damping(1)
    if 2 in comps:
        out[2] = centre[2] - COURANT * (MACH * z_slope(2) + z_slope(1)) - damping(2)
    if 3 in comps:
        out[3] = centre[3] - COURANT * (MACH * z_slope(3) + y_slope(1)) - damping(3)
    return out


def pack_body(
    halo, me_ref, ids_hbm, disp_hbm, flow_hbm, wt_hbm,
    near_ref, far_ref, own_ref, row_ref, ids_ref, flow_ref, wt_ref, sem,
):
    odd = me_ref[0] % 2 == 1
    comps, cells, width = flow_hbm.shape
    count = wt_hbm.shape[0]
    halves = wt_hbm.shape[2] // width
    deep = 2 * halo
    copies = [
        (flow_hbm.at[:, pl.ds(0, halo)], flow_ref.at[0]),
        (flow_hbm.at[:, pl.ds(cells - halo, halo)], flow_ref.at[1]),
        (wt_hbm.at[:, pl.ds(0, deep)], wt_ref.at[0]),
        (wt_hbm.at[:, pl.ds(cells - deep, deep)], wt_ref.at[1]),
        (ids_hbm, ids_ref),
        (disp_hbm, row_ref),
    ]
    copies = [pltpu.make_async_copy(src, dst, sem.at[i]) for i, (src, dst) in enumerate(copies)]
    for copy in copies:
        copy.start()
    for copy in copies:
        copy.wait()
    at = 0
    for c in range(comps):
        head, tail = flow_ref[0, c], flow_ref[1, c]
        near_ref[at : at + halo, :] = jnp.where(odd, head, tail)
        far_ref[at : at + halo, :] = jnp.where(odd, tail, head)
        at += halo
    for k in range(count):
        head = wt_ref[0, k].astype(jnp.float32)[0:halo]
        tail = wt_ref[1, k].astype(jnp.float32)[halo:deep]
        near = jnp.where(odd, head, tail)
        far = jnp.where(odd, tail, head)
        for h in range(halves):
            near_ref[at : at + halo, :] = near[:, h * width : (h + 1) * width]
            far_ref[at : at + halo, :] = far[:, h * width : (h + 1) * width]
            at += halo
    row = lax.broadcasted_iota(jnp.int32, (SUB, width), 0)
    ids = jnp.full((SUB, width), -1, jnp.int32)
    for k in range(count):
        ids = jnp.where(row == k, ids_ref[k], ids)
    ids = ids.astype(jnp.float32)
    near_ref[at : at + SUB, :] = ids
    far_ref[at : at + SUB, :] = ids
    own_ref[...] = ids[:, 0:LANES]


def wall_body(
    halo, me_ref, ids_ref, mine_ref, theirs_ref, own_ref, near_ref, far_ref, flow_ref, wt_ref, pivots_ref,
    wall_ref, permuted_ref, ping, pong,
):
    me = me_ref[0]
    odd = me % 2
    is_odd = odd == 1
    chips = mine_ref.shape[0]
    comps, cells, width = flow_ref.shape
    count, _, block = wt_ref.shape
    halves = block // width
    ids_at = halo * (comps + count * halves)

    slot = lax.broadcasted_iota(jnp.int32, (SUB * 3, 2 * chips), 1)
    chip = (me // 2) ^ (slot % chips)
    core = odd ^ (slot // chips)
    block_of = (2 * chip + core).astype(jnp.float32)
    ids = jnp.concatenate(
        [own_ref[:, 0:1], near_ref[ids_at : ids_at + SUB, 0:1], far_ref[ids_at : ids_at + SUB, 0:1]],
        axis=0,
    )
    choose = (ids == block_of).astype(jnp.bfloat16)
    table = jnp.concatenate([mine_ref[...], theirs_ref[...]], axis=0).astype(jnp.bfloat16)
    picked = jnp.dot(choose, table, preferred_element_type=jnp.float32)

    own = jnp.zeros((cells, LANES), jnp.float32)
    edge = [jnp.zeros((halo, LANES), jnp.float32) for _ in range(2)]
    for k in range(count):
        weights = wt_ref[k].astype(jnp.float32)
        for q in range(0, block, LANES):
            own += weights[:, q : q + LANES] * picked[k : k + 1, q : q + LANES]
            rows = halo * (comps + k * halves + q // width)
            for e, ref in enumerate((near_ref, far_ref)):
                edge[e] += (
                    ref[rows : rows + halo, q % width : q % width + LANES]
                    * picked[SUB * (e + 1) + k : SUB * (e + 1) + k + 1, q : q + LANES]
                )
    own = jnp.sum(own, axis=1, keepdims=True)
    near, far = [jnp.sum(e, axis=1, keepdims=True) for e in edge]

    def beside(load):
        group = lane_index((1, LANES)) // GROUP
        pressure, along, normal = [load(c)[:, 0:LANES] for c in (1, 2, 3)]
        packed = jnp.where(group == 1, pltpu.roll(along, GROUP, 1), pressure)
        return jnp.where(group == 2, pltpu.roll(normal, 2 * GROUP, 1), packed)

    at_near, at_far = [
        beside(lambda c: ref[c * halo : (c + 1) * halo, :]) for ref in (near_ref, far_ref)
    ]
    first = lane_index((1, LANES)) == 2 * GROUP
    parts = [
        (0, jnp.where(is_odd, near, far), jnp.where(is_odd, at_near, at_far)),
        (halo, own, beside(lambda c: flow_ref[c])),
        (halo + cells, jnp.where(is_odd, far, near), jnp.where(is_odd, at_far, at_near)),
    ]
    for at, column, part in parts:
        rows = column.shape[0]
        column = jnp.broadcast_to(column, (rows, LANES))
        wall_ref[at : at + rows, :] = column
        ping[SUB + at : SUB + at + rows, :] = jnp.where(first, column, part)

    extent = cells + 2 * halo
    src, dst = ping, pong
    for index in range(ITERS):
        at, rows = (SUB, extent) if index < ITERS - 1 else (SUB + halo, cells)
        lane = lane_index((rows, LANES))
        group = lane // GROUP
        height = lane % GROUP
        centre = src[at : at + rows, :]
        z_plus, z_minus = [src[at + o : at + o + rows, :] for o in (1, -1)]
        y_plus = pltpu.roll(centre, LANES - 1, 1)
        y_minus = jnp.where(height >= 1, pltpu.roll(centre, 1, 1), 0.0)
        far_y = pltpu.roll(centre, LANES - 2, 1) + jnp.where(height >= 2, pltpu.roll(centre, 2, 1), 0.0)
        far_z = src[at + 2 : at + 2 + rows, :] + src[at - 2 : at - 2 + rows, :]
        damping = DISSIPATION * (
            far_y + far_z - 4.0 * (z_plus + z_minus + y_plus + y_minus) + 12.0 * centre
        )
        z_slope = 0.5 * (z_plus - z_minus)
        other_y = 0.5 * (
            pltpu.roll(centre, 2 * GROUP - 1, 1)
            - jnp.where(height >= 1, pltpu.roll(centre, 2 * GROUP + 1, 1), 0.0)
        )
        cross = jnp.where(group == 0, pltpu.roll(z_slope, LANES - GROUP, 1) + other_y, other_y)
        cross = jnp.where(group == 1, pltpu.roll(z_slope, GROUP, 1), cross)
        value = centre - COURANT * (MACH * z_slope + cross) - damping
        if index < ITERS - 1:
            dst[at : at + rows, :] = jnp.where(group == 3, 0.0, value)
        src, dst = dst, src
    push = (FACE_AREA * value[:, 0:1]).astype(jnp.bfloat16).astype(jnp.float32)
    push = jnp.broadcast_to(push, (cells, LANES))

    pivot = pivots_ref[...]
    row = jnp.right_shift(pivot, LANES.bit_length() - 1)
    lane = jnp.bitwise_and(pivot, LANES - 1)
    got = jnp.zeros(pivot.shape, jnp.float32)
    for k in range(count):
        weights = wt_ref[k].astype(jnp.float32)
        for q in range(block // LANES):
            term = jnp.sum(weights[:, q * LANES : (q + 1) * LANES] * push, axis=0, keepdims=True)
            source = jnp.take_along_axis(jnp.broadcast_to(term, pivot.shape), lane, axis=1)
            got = jnp.where(row == ids_ref[k] * (block // LANES) + q, source, got)
    permuted_ref[...] = got


def flow_body(
    halo, me_ref, near_ref, far_ref, flow_hbm, wall_ref, front_hbm, out_ref, tail_ref, ping, pong, sem
):
    left = front_hbm.shape[1] - tail_ref.shape[1]
    fetch = pltpu.make_async_copy(front_hbm.at[:, pl.ds(left, tail_ref.shape[1])], tail_ref, sem.at[0])
    fetch.start()
    is_odd = me_ref[0] % 2 == 1
    comps, cells, width = flow_hbm.shape
    middle = SUB + halo
    field = pltpu.make_async_copy(flow_hbm, ping.at[:, pl.ds(middle, cells)], sem.at[1])
    field.start()
    lane = lane_index((1, width))
    for c in range(comps):
        near = near_ref[c * halo : (c + 1) * halo, :]
        far = far_ref[c * halo : (c + 1) * halo, :]
        for at, part in ((0, jnp.where(is_odd, near, far)), (halo + cells, jnp.where(is_odd, far, near))):
            if c == comps - 1:
                part = jnp.where(lane == 0, wall_ref[at : at + halo, 0:1], part)
            ping[c, SUB + at : SUB + at + halo, :] = part
    field.wait()
    wall = wall_ref[halo : halo + cells, :]
    normal = ping[comps - 1, middle : middle + cells, 0:LANES]
    ping[comps - 1, middle : middle + cells, 0:LANES] = jnp.where(lane_index((1, LANES)) == 0, wall, normal)
    src, dst = ping, pong
    extent = cells + 2 * halo
    for index in range(ITERS):
        last = index == ITERS - 1
        first = halo if last else 0
        total = cells if last else extent
        step = 16
        for at in range(first, first + total, step):
            base = SUB + at
            out = sweep(lambda c, o: src[c, base + o : base + o + step, :], (0, 1, 2, 3))
            for c, value in out.items():
                if last:
                    out_ref[c, at - halo : at - halo + step, :] = value
                else:
                    dst[c, base : base + step, :] = value
        src, dst = dst, src
    fetch.wait()


def spread_rows(columns, row_of):
    return [jnp.broadcast_to(row_of(c), (SUB, LANES)) for c in range(columns // LANES)]


def front_product(front_ref, spread):
    rows, columns = front_ref.shape
    out = []
    for top in range(0, rows, LANES):
        parts = []
        for at in range(top, top + LANES, SUB):
            total = None
            for c in range(columns // LANES):
                term = front_ref[at : at + SUB, c * LANES : (c + 1) * LANES] * spread[c]
                total = term if total is None else total + term
            parts.append(total)
        out.append(jnp.sum(jnp.concatenate(parts, axis=0).T, axis=0, keepdims=True))
    return jnp.concatenate(out, axis=1)


def lower_body(parts, *refs):
    front_ref, out_ref, permuted = refs[parts:]
    total = refs[0][...]
    for ref in refs[1:parts]:
        total = total + ref[...]
    permuted[...] = total
    spread = spread_rows(front_ref.shape[1], lambda c: permuted[c : c + 1, :])
    result = front_product(front_ref, spread)
    out_ref[...] = jnp.broadcast_to(result[None], out_ref.shape)


def upper_body(
    sections, me_ref, parts_ref, disp_hbm, tail_ref, front_hbm, out_ref, disp_ref, head_ref, total, sem
):
    me = me_ref[0]
    block = parts_ref.shape[2]
    domains = parts_ref.shape[0] // sections
    heads = head_ref.shape[0]
    copies = [
        pltpu.make_async_copy(
            front_hbm.at[:, pl.ds(b * block, block)], head_ref.at[b], sem.at[b]
        )
        for b in range(heads)
    ]
    own = pltpu.make_async_copy(disp_hbm, disp_ref, sem.at[heads])
    own.start()
    for b in reversed(range(heads)):
        pl.when(b >= me)(copies[b].start)
    total[...] = jnp.zeros_like(total)
    for b in reversed(range(domains)):

        def add(b=b):
            if b < heads:
                copies[b].wait()
            rows = []
            for q in range(0, block, LANES):
                first = (domains - 1 - b) * sections
                part = parts_ref[first, :, q : q + LANES]
                for s in range(1, sections):
                    part = part + parts_ref[first + s, :, q : q + LANES]
                rows.append(jnp.broadcast_to(part, (SUB, LANES)))
            for at in range(0, block, SUB):
                value = total[at : at + SUB, :]
                for i, row in enumerate(rows):
                    if b < heads:
                        front = head_ref[b, at : at + SUB, i * LANES : (i + 1) * LANES]
                    else:
                        left = (b - heads) * block + i * LANES
                        front = tail_ref[at : at + SUB, left : left + LANES]
                    value = value + front * row
                total[at : at + SUB, :] = value

        pl.when(b >= me)(add)
    solved = [
        jnp.sum(total[at : at + LANES, :].T, axis=0, keepdims=True) for at in range(0, block, LANES)
    ]
    own.wait()
    out_ref[...] = 0.5 * disp_ref[...] + 0.5 * jnp.concatenate(solved, axis=1)


VMEM = pl.BlockSpec(memory_space=pltpu.VMEM)
SMEM = pl.BlockSpec(memory_space=pltpu.SMEM)
HBM = pl.BlockSpec(memory_space=pltpu.HBM)

COVER = 20_000_000_000

TAIL_BYTES = 2 << 20


def call(body, in_specs, out_shape, scratch, cost, limit):
    many = isinstance(out_shape, tuple)
    return pl.pallas_call(
        body,
        out_shape=out_shape,
        in_specs=in_specs,
        out_specs=(VMEM,) * len(out_shape) if many else VMEM,
        scratch_shapes=scratch,
        compiler_params=pltpu.CompilerParams(vmem_limit_bytes=limit),
        cost_estimate=pl.CostEstimate(flops=cost[0], bytes_accessed=cost[1], transcendentals=0),
    )


def in_hbm(array):
    return pltpu.with_memory_space_constraint(array, pltpu.HBM)


def f32(*shape):
    return jax.ShapeDtypeStruct(shape, jnp.float32)


def fast_shards(disp_coarse, support_ids, rbf_weights, flow, pivots, lower_inverse, upper_inverse):
    block = disp_coarse.shape[0]
    sections, domains = lax.axis_size("sec"), lax.axis_size("dom")
    chips = domains // 2
    halo = REACH * ITERS
    me = lax.axis_index("dom").astype(jnp.int32).reshape(1)
    ids = support_ids[0, 0]
    weights = jnp.swapaxes(rbf_weights[0, 0], 1, 2)
    field = flow[0]
    count, cells, _ = weights.shape
    comps, _, width = field.shape

    def across(array, k):
        return lax.ppermute(array, "dom", [(i, i ^ (2 * k)) for i in range(domains)])

    def partner(array):
        return lax.ppermute(array, "dom", [(i, i ^ 1) for i in range(domains)])

    def neighbour(array):
        pairs = [(i, (i + 1) % domains if i % 2 else (i - 1) % domains) for i in range(domains)]
        return lax.ppermute(array, "dom", pairs)

    row = disp_coarse.reshape(1, block)
    rows = halo * comps + halo * count * (block // width) + SUB
    near, far, own, mine = call(
        functools.partial(pack_body, halo),
        [SMEM] + [HBM] * 4,
        (f32(rows, width), f32(rows, width), f32(SUB, LANES), f32(1, block)),
        [
            pltpu.SMEM((count,), jnp.int32),
            pltpu.VMEM((2, comps, halo, width), jnp.float32),
            pltpu.VMEM((2, count, 2 * halo, block), weights.dtype),
            pltpu.SemaphoreType.DMA((6,)),
        ],
        (COVER, 400_000),
        4 << 20,
    )(me, *[in_hbm(x) for x in (ids, row, field, weights)])
    far = neighbour(far)
    near = partner(near)
    others = []
    for k in range(1, chips):
        others.append(across(row if k == chips - 1 else mine, k))
    mine = jnp.concatenate([mine] + others, axis=0)
    theirs = partner(mine)

    extent = cells + 2 * halo
    pivot_rows = pivots.reshape(-1, LANES)
    wall, permuted = call(
        functools.partial(wall_body, halo),
        [SMEM, SMEM] + [VMEM] * 8,
        (f32(extent, LANES), f32(*pivot_rows.shape)),
        [pltpu.VMEM((extent + 2 * SUB, LANES), jnp.float32)] * 2,
        (COVER, 40_000_000),
        8 << 20,
    )(me, ids, mine, theirs, own, near, far, field, weights, pivot_rows)

    pair = permuted + partner(permuted)
    pieces = [pair] + [across(pair, k) for k in range(chips - 1, 0, -1)]
    tails = max(1, min(domains - 1, TAIL_BYTES // (4 * block * block)))
    new_flow, tail = call(
        functools.partial(flow_body, halo),
        [SMEM, VMEM, VMEM, HBM, VMEM, HBM],
        (f32(comps, cells, width), f32(block, tails * block)),
        [pltpu.VMEM((comps, extent + 2 * SUB, width), jnp.float32)] * 2
        + [pltpu.SemaphoreType.DMA((2,))],
        (COVER, 4_000_000),
        8 << 20,
    )(me, near, far, in_hbm(field), wall, in_hbm(upper_inverse))

    lower = call(
        functools.partial(lower_body, len(pieces)),
        [VMEM] * (len(pieces) + 1),
        f32(sections * domains, 1, block),
        [pltpu.VMEM(pivot_rows.shape, jnp.float32)],
        (COVER, 1_000_000),
        4 << 20,
    )(*pieces, lower_inverse)
    order = [s * domains + d for d in reversed(range(domains)) for s in range(sections)]
    middle = lax.all_to_all(
        lower, ("sec", "dom"), 0, 0, axis_index_groups=[order], tiled=True
    )
    new_disp = call(
        functools.partial(upper_body, sections),
        [SMEM, VMEM, HBM, VMEM, HBM],
        f32(1, block),
        [
            pltpu.VMEM((1, block), jnp.float32),
            pltpu.VMEM((domains - tails, block, block), jnp.float32),
            pltpu.VMEM((block, LANES), jnp.float32),
            pltpu.SemaphoreType.DMA((domains - tails + 1,)),
        ],
        (COVER, 1_000_000),
        12 << 20,
    )(me, middle, in_hbm(row), tail, in_hbm(upper_inverse))
    return (new_flow[None], new_disp.reshape(block))


def fits(mesh):
    chips, odd = divmod(mesh.shape["dom"], 2)
    return odd == 0 and chips & (chips - 1) == 0 and 1 < chips <= 8


def body_for(mesh):
    def body(disp_coarse, support_ids, rbf_weights, flow, pivots, lower_inverse, upper_inverse):
        args = (disp_coarse, support_ids, rbf_weights, flow, pivots, lower_inverse, upper_inverse)
        block = disp_coarse.shape[0]
        cells, width = flow.shape[2:]
        halo = REACH * ITERS
        small = (
            block % width == 0
            and width % LANES == 0
            and cells % (4 * halo) == 0
            and halo == SUB
            and 2 * halo < GROUP
            and flow.shape[1] == 4
            and pivots.shape[0] % (SUB * LANES) == 0
            and support_ids.shape[2] <= SUB
        )
        return fast_shards(*args) if fits(mesh) and small else shards(*args)

    return body


def solution(mesh):
    return jax.shard_map(
        body_for(mesh),
        mesh=mesh,
        in_specs=(
            P("dom"),
            P("sec", "dom", None),
            P("sec", "dom", None, None, None),
            P("sec", None, "dom", None),
            P(),
            P("dom", None),
            P("dom", None),
        ),
        out_specs=(P("sec", None, "dom", None), P("dom")),
        check_vma=False,
    )
```

profile of v0, /device:TPU:0, one launch (start us, length us, event | category | flops | bytes accessed | tf_op | source)
XLA Modules:
  0.0 42.0 jit_solution(888749349841484077)
XLA Ops:
  0.6 5.1 %collective-permute-start.4 = (f32[1,512]{1,0:T(1,128)}, f32[1,512]{1,0:T(1,128)S(1)}, u32[]{:S(2)}, u32[]{:S(2)}) collective-permute-start(f32[1,512]{1,0:T(1,128)} %bitcast.20), channel_id=1, source_target_pairs={{0,6},{1,7},{2,4},{3,5},{4,2},{5,3},{6,0},{7,1},{8,14},{9,15},{10,... | collective-permute-start | bytes 6152 | tf_op jit(solution)/shard_map/ppermute | solution.py:462
  5.8 0.0 slice-start
  5.8 1.1 %shard_map.86 = (f32[104,256]{1,0:T(8,128)S(1)}, f32[104,256]{1,0:T(8,128)S(1)}, f32[8,128]{1,0:T(8,128)S(1)}, f32[1,512]{1,0:T(1,128)S(1)}) custom-call(s32[1]{0:T(128)} %bitcast.me_ref, s32[4]{0:T(128)} %bitcast.18, f32[1,512]{1,0:T(1,128)} %bitcast.21, f32[4,64,256]{2,1,0:T(8,128)} %bitcast.14, bf16[4,64,512]{2,1,0:T(8,128)(2,1)} %bitcast.12), custom_call_target="tpu_custom_call" | custom-call | flops 20000000000 | bytes 400000 | tf_op jit(solution)/shard_map/pallas_call | solution.py:473
  6.9 0.1 collective-permute-start.3
  7.0 0.6 %collective-permute-start.2 = (f32[1,512]{1,0:T(1,128)S(1)}, f32[1,512]{1,0:T(1,128)S(1)}, u32[]{:S(2)}, u32[]{:S(2)}) collective-permute-start(f32[1,512]{1,0:T(1,128)S(1)} %get-tuple-element.12), channel_id=1, source_target_pairs={{0,2},{1,3},{2,0},{3,1},{4,6},{5,7},{6,4},{7,5},{8,10},{9,11},{10,... | collective-permute-start | bytes 6152 | tf_op jit(solution)/shard_map/ppermute | solution.py:462
  7.6 0.0 collective-permute-start
  7.6 3.9 %collective-permute-start.1 = (f32[104,256]{1,0:T(8,128)S(1)}, f32[104,256]{1,0:T(8,128)S(1)}, u32[]{:S(2)}, u32[]{:S(2)}) collective-permute-start(f32[104,256]{1,0:T(8,128)S(1)} %get-tuple-element.11), channel_id=1, source_target_pairs={{0,7},{1,2},{2,1},{3,4},{4,3},{5,6},{6,5},{7,0},{8,15},{9,10},{10,... | collective-permute-start | bytes 319496 | tf_op jit(solution)/shard_map/ppermute | solution.py:469
  11.5 0.0 collective-permute-done.4
  11.5 0.1 collective-permute-done.3
  11.6 0.0 collective-permute-done.2
  11.6 0.1 collective-permute-start.5
  11.7 1.2 %collective-permute-done.5.theirs_ref = f32[4,512]{1,0:T(4,128)S(1)} collective-permute-done((f32[4,512]{1,0:T(4,128)S(1)}, f32[4,512]{1,0:T(4,128)S(1)}, u32[]{:S(2)}, u32[]{:S(2)}) %collective-permute-start.5) | collective-permute-done | bytes 8224 | tf_op jit(solution)/shard_map/ppermute | solution.py:465
  12.9 0.0 collective-permute-done.near_ref
  12.9 1.9 %collective-permute-done.1.far_ref = f32[104,256]{1,0:T(8,128)S(1)} collective-permute-done((f32[104,256]{1,0:T(8,128)S(1)}, f32[104,256]{1,0:T(8,128)S(1)}, u32[]{:S(2)}, u32[]{:S(2)}) %collective-permute-start.1) | collective-permute-done | bytes 106528 | tf_op jit(solution)/shard_map/ppermute | solution.py:469
  14.8 0.0 copy-done
  14.8 0.0 copy-done.2
  14.8 0.0 slice-start.1
  14.8 1.7 %shard_map.87 = (f32[80,128]{1,0:T(8,128)S(1)}, f32[32,128]{1,0:T(8,128)S(1)}) custom-call(s32[1]{0:T(128)} %bitcast.me_ref, s32[4]{0:T(128)S(1)} %bitcast.19, f32[4,512]{1,0:T(4,128)S(1)} %pad_maximum_fusion.mine_ref, f32[4,512]{1,0:T(4,128)S(1)} %collective-permute-done.5.theirs_ref, f32[8,128]{1,0:T(8,128)S(1)} %get-tuple-element.13.own_ref, ...), custom_call_target="tpu_custom_call" | custom-call | flops 20000000000 | bytes 40000000 | tf_op jit(solution)/shard_map/pallas_call | solution.py:496
  16.6 0.1 collective-permute-start.6
  16.6 1.2 %collective-permute-done.6 = f32[32,128]{1,0:T(8,128)S(1)} collective-permute-done((f32[32,128]{1,0:T(8,128)S(1)}, f32[32,128]{1,0:T(8,128)S(1)}, u32[]{:S(2)}, u32[]{:S(2)}) %collective-permute-start.6) | collective-permute-done | bytes 16416 | tf_op jit(solution)/shard_map/ppermute | solution.py:465
  17.8 2.7 %collective-permute-start.7 = (f32[32,128]{1,0:T(8,128)S(1)}, f32[32,128]{1,0:T(8,128)S(1)}, u32[]{:S(2)}, u32[]{:S(2)}) collective-permute-start(f32[32,128]{1,0:T(8,128)S(1)} %add.3.refs_0_), channel_id=1, source_target_pairs={{0,6},{1,7},{2,4},{3,5},{4,2},{5,3},{6,0},{7,1},{8,14},{9,15},{10,... | collective-permute-start | bytes 49160 | tf_op jit(solution)/shard_map/ppermute | solution.py:462
  20.5 0.0 collective-permute-start.8
  20.5 1.7 %collective-permute-start.9 = (f32[32,128]{1,0:T(8,128)S(1)}, f32[32,128]{1,0:T(8,128)S(1)}, u32[]{:S(2)}, u32[]{:S(2)}) collective-permute-start(f32[32,128]{1,0:T(8,128)S(1)} %add.3.refs_0_), channel_id=1, source_target_pairs={{0,2},{1,3},{2,0},{3,1},{4,6},{5,7},{6,4},{7,5},{8,10},{9,11},{10,... | collective-permute-start | bytes 49160 | tf_op jit(solution)/shard_map/ppermute | solution.py:462
  22.2 1.2 %collective-permute-done.7.refs_1_ = f32[32,128]{1,0:T(8,128)S(1)} collective-permute-done((f32[32,128]{1,0:T(8,128)S(1)}, f32[32,128]{1,0:T(8,128)S(1)}, u32[]{:S(2)}, u32[]{:S(2)}) %collective-permute-start.7) | collective-permute-done | bytes 16416 | tf_op jit(solution)/shard_map/ppermute | solution.py:462
  23.4 1.8 %collective-permute-done.8.refs_2_ = f32[32,128]{1,0:T(8,128)S(1)} collective-permute-done((f32[32,128]{1,0:T(8,128)S(1)}, f32[32,128]{1,0:T(8,128)S(1)}, u32[]{:S(2)}, u32[]{:S(2)}) %collective-permute-start.8) | collective-permute-done | bytes 16416 | tf_op jit(solution)/shard_map/ppermute | solution.py:462
  25.1 0.0 collective-permute-done.9.refs_3_
  25.2 0.0 slice-done.1
  25.2 1.3 %shard_map.89 = f32[32,1,512]{2,1,0:T(1,128)} custom-call(f32[32,128]{1,0:T(8,128)S(1)} %add.3.refs_0_, f32[32,128]{1,0:T(8,128)S(1)} %collective-permute-done.7.refs_1_, f32[32,128]{1,0:T(8,128)S(1)} %collective-permute-done.8.refs_2_, f32[32,128]{1,0:T(8,128)S(1)} %collective-permute-done.9.refs_3_, f32[512,4096]{1,0:T(8,128)S(1)} %bitcast.11), custom_call_target="tpu_custom_call" | custom-call | flops 20000000000 | bytes 1000000 | tf_op jit(solution)/shard_map/pallas_call | solution.py:518
  26.4 4.3 %all-to-all-start = ((f32[32,1,512]{2,1,0:T(1,128)}), f32[32,1,512]{2,1,0:T(1,128)S(1)}, u32[]{:S(2)}, u32[]{:S(2)}) async-start(f32[32,1,512]{2,1,0:T(1,128)} %shard_map.89), calls=%async_computation | async-start | bytes 131072 | tf_op jit(solution)/shard_map/all_to_all | solution.py:527
  30.7 4.6 %shard_map.88 = (f32[4,64,256]{2,1,0:T(8,128)}, f32[512,1024]{1,0:T(8,128)S(1)}) custom-call(s32[1]{0:T(128)} %bitcast.me_ref, f32[104,256]{1,0:T(8,128)S(1)} %collective-permute-done.near_ref, f32[104,256]{1,0:T(8,128)S(1)} %collective-permute-done.1.far_ref, f32[4,64,256]{2,1,0:T(8,128)} %bitcast.15, f32[80,128]{1,0:T(8,128)S(1)} %get-tuple-element.14.wall_ref, ...), custom_call_target="tpu_custom_call" | custom-call | flops 20000000000 | bytes 4000000 | tf_op jit(solution)/shard_map/pallas_call | solution.py:508
  35.3 3.0 %all-to-all-done.parts_ref = f32[32,1,512]{2,1,0:T(1,128)S(1)} async-done(((f32[32,1,512]{2,1,0:T(1,128)}), f32[32,1,512]{2,1,0:T(1,128)S(1)}, u32[]{:S(2)}, u32[]{:S(2)}) %all-to-all-start) | async-done | bytes 65568 | tf_op jit(solution)/shard_map/all_to_all | solution.py:527
  38.3 3.7 %shard_map.90 = f32[1,512]{1,0:T(1,128)} custom-call(s32[1]{0:T(128)} %bitcast.me_ref, f32[32,1,512]{2,1,0:T(1,128)S(1)} %all-to-all-done.parts_ref, f32[1,512]{1,0:T(1,128)} %bitcast.22, f32[512,1024]{1,0:T(8,128)S(1)} %get-tuple-element.17.tail_ref, f32[512,4096]{1,0:T(8,128)} %front_hbm.3), custom_call_target="tpu_custom_call" | custom-call | flops 20000000000 | bytes 1000000 | tf_op jit(solution)/shard_map/pallas_call | solution.py:530
  (10 shorter events, 0.0 us)
Async XLA Ops:
  0.6 10.9 %collective-permute-start.4 = (f32[1,512]{1,0:T(1,128)}, f32[1,512]{1,0:T(1,128)S(1)}, u32[]{:S(2)}, u32[]{:S(2)}) collective-permute-start(f32[1,512]{1,0:T(1,128)} %bitcast.20), channel_id=1, source_target_pairs={{0,6},{1,7},{2,4},{3,5},{4,2},{5,3},{6,0},{7,1},{8,14},{9,15},{10,... | collective-permute-start | bytes 6152 | tf_op jit(solution)/shard_map/ppermute | solution.py:462
  5.8 9.0 %copy-start = (bf16[1,1,4,512,64]{3,4,2,1,0:T(8,128)(2,1)S(1)}, bf16[1,1,4,512,64]{3,4,2,1,0:T(8,128)(2,1)}, u32[]{:S(2)}) copy-start(bf16[1,1,4,512,64]{3,4,2,1,0:T(8,128)(2,1)} %param.9) | copy-start | bytes 786436
  5.8 9.0 %copy-start.1 = (f32[1,4,64,256]{3,2,1,0:T(8,128)S(1)}, f32[1,4,64,256]{3,2,1,0:T(8,128)}, u32[]{:S(2)}) copy-start(f32[1,4,64,256]{3,2,1,0:T(8,128)} %param.10) | copy-start | bytes 786436
  5.8 9.0 %copy-start.2 = (s32[4096]{0:T(1024)S(1)}, s32[4096]{0:T(1024)}, u32[]{:S(2)}) copy-start(s32[4096]{0:T(1024)} %param.11) | copy-start | bytes 49156
  5.8 9.0 %copy-start.3 = (s32[1,1,4]{2,1,0:T(1,128)S(1)}, s32[1,1,4]{2,1,0:T(1,128)}, u32[]{:S(2)}) copy-start(s32[1,1,4]{2,1,0:T(1,128)} %param.8) | copy-start | bytes 52
  5.8 19.4 %slice-start = ((s8[8388608]{0:T(1024)(128)(4,1)}), s8[4194304]{0:T(1024)(128)(4,1)S(1)}, s32[]{:S(2)}) async-start(s8[8388608]{0:T(1024)(128)(4,1)} %bitcast.10), calls=%async_computation.1 | async-start | bytes 8388608
  6.9 4.7 %collective-permute-start.3 = (f32[1,512]{1,0:T(1,128)S(1)}, f32[1,512]{1,0:T(1,128)S(1)}, u32[]{:S(2)}, u32[]{:S(2)}) collective-permute-start(f32[1,512]{1,0:T(1,128)S(1)} %get-tuple-element.12), channel_id=1, source_target_pairs={{0,4},{1,5},{2,6},{3,7},{4,0},{5,1},{6,2},{7,3},{8,12},{9,13},{10,... | collective-permute-start | bytes 6152 | tf_op jit(solution)/shard_map/ppermute | solution.py:462
  7.0 4.6 %collective-permute-start.2 = (f32[1,512]{1,0:T(1,128)S(1)}, f32[1,512]{1,0:T(1,128)S(1)}, u32[]{:S(2)}, u32[]{:S(2)}) collective-permute-start(f32[1,512]{1,0:T(1,128)S(1)} %get-tuple-element.12), channel_id=1, source_target_pairs={{0,2},{1,3},{2,0},{3,1},{4,6},{5,7},{6,4},{7,5},{8,10},{9,11},{10,... | collective-permute-start | bytes 6152 | tf_op jit(solution)/shard_map/ppermute | solution.py:462
  7.6 5.2 %collective-permute-start = (f32[104,256]{1,0:T(8,128)S(1)}, f32[104,256]{1,0:T(8,128)S(1)}, u32[]{:S(2)}, u32[]{:S(2)}) collective-permute-start(f32[104,256]{1,0:T(8,128)S(1)} %get-tuple-element.10), channel_id=1, source_target_pairs={{0,1},{1,0},{2,3},{3,2},{4,5},{5,4},{6,7},{7,6},{8,9},{9,8},{10,11... | collective-permute-start | bytes 319496 | tf_op jit(solution)/shard_map/ppermute | solution.py:465
  7.6 7.2 %collective-permute-start.1 = (f32[104,256]{1,0:T(8,128)S(1)}, f32[104,256]{1,0:T(8,128)S(1)}, u32[]{:S(2)}, u32[]{:S(2)}) collective-permute-start(f32[104,256]{1,0:T(8,128)S(1)} %get-tuple-element.11), channel_id=1, source_target_pairs={{0,7},{1,2},{2,1},{3,4},{4,3},{5,6},{6,5},{7,0},{8,15},{9,10},{10,... | collective-permute-start | bytes 319496 | tf_op jit(solution)/shard_map/ppermute | solution.py:469
  11.6 1.2 %collective-permute-start.5 = (f32[4,512]{1,0:T(4,128)S(1)}, f32[4,512]{1,0:T(4,128)S(1)}, u32[]{:S(2)}, u32[]{:S(2)}) collective-permute-start(f32[4,512]{1,0:T(4,128)S(1)} %pad_maximum_fusion.mine_ref), channel_id=1, source_target_pairs={{0,1},{1,0},{2,3},{3,2},{4,5},{5,4},{6,7},{7,6},{8,9},{9,8},{10,11... | collective-permute-start | bytes 24584 | tf_op jit(solution)/shard_map/ppermute | solution.py:465
  14.8 10.3 %slice-start.1 = ((s8[8388608]{0:T(1024)(128)(4,1)}), s8[4194304]{0:T(1024)(128)(4,1)S(1)}, s32[]{:S(2)}) async-start(s8[8388608]{0:T(1024)(128)(4,1)} %bitcast.10), calls=%async_computation.2 | async-start | bytes 8388608
  16.6 1.2 %collective-permute-start.6 = (f32[32,128]{1,0:T(8,128)S(1)}, f32[32,128]{1,0:T(8,128)S(1)}, u32[]{:S(2)}, u32[]{:S(2)}) collective-permute-start(f32[32,128]{1,0:T(8,128)S(1)} %get-tuple-element.16), channel_id=1, source_target_pairs={{0,1},{1,0},{2,3},{3,2},{4,5},{5,4},{6,7},{7,6},{8,9},{9,8},{10,11... | collective-permute-start | bytes 49160 | tf_op jit(solution)/shard_map/ppermute | solution.py:465
  17.8 5.6 %collective-permute-start.7 = (f32[32,128]{1,0:T(8,128)S(1)}, f32[32,128]{1,0:T(8,128)S(1)}, u32[]{:S(2)}, u32[]{:S(2)}) collective-permute-start(f32[32,128]{1,0:T(8,128)S(1)} %add.3.refs_0_), channel_id=1, source_target_pairs={{0,6},{1,7},{2,4},{3,5},{4,2},{5,3},{6,0},{7,1},{8,14},{9,15},{10,... | collective-permute-start | bytes 49160 | tf_op jit(solution)/shard_map/ppermute | solution.py:462
  20.5 4.6 %collective-permute-start.8 = (f32[32,128]{1,0:T(8,128)S(1)}, f32[32,128]{1,0:T(8,128)S(1)}, u32[]{:S(2)}, u32[]{:S(2)}) collective-permute-start(f32[32,128]{1,0:T(8,128)S(1)} %add.3.refs_0_), channel_id=1, source_target_pairs={{0,4},{1,5},{2,6},{3,7},{4,0},{5,1},{6,2},{7,3},{8,12},{9,13},{10,... | collective-permute-start | bytes 49160 | tf_op jit(solution)/shard_map/ppermute | solution.py:462
  20.5 4.6 %collective-permute-start.9 = (f32[32,128]{1,0:T(8,128)S(1)}, f32[32,128]{1,0:T(8,128)S(1)}, u32[]{:S(2)}, u32[]{:S(2)}) collective-permute-start(f32[32,128]{1,0:T(8,128)S(1)} %add.3.refs_0_), channel_id=1, source_target_pairs={{0,2},{1,3},{2,0},{3,1},{4,6},{5,7},{6,4},{7,5},{8,10},{9,11},{10,... | collective-permute-start | bytes 49160 | tf_op jit(solution)/shard_map/ppermute | solution.py:462
  26.4 11.9 %all-to-all-start = ((f32[32,1,512]{2,1,0:T(1,128)}), f32[32,1,512]{2,1,0:T(1,128)S(1)}, u32[]{:S(2)}, u32[]{:S(2)}) async-start(f32[32,1,512]{2,1,0:T(1,128)} %shard_map.89), calls=%async_computation | async-start | bytes 131072 | tf_op jit(solution)/shard_map/all_to_all | solution.py:527
where the time goes:
time: 42.2 us; the launch traced here: 42 us
  starting transfers between devices  18.5 us (44%)
  Pallas kernels  12.4 us (29%)
  waiting for transfers between devices  10.3 us (24%)
  between operations  0.74 us (2%)
    ppermute x6, starting transfers between devices, across(): return lax.ppermute(array, 'dom', [(i, i ^ 2 * k) for i in range(domains)])  10.2 us
    pallas_call x1, Pallas kernels, fast_shards(): call(functools.partial(flow_body, halo), [SMEM, VMEM, VMEM, HBM, VMEM, HB...  4.56 us
    all_to_all x1, starting transfers between devices, fast_shards(): lax.all_to_all(lower, ('sec', 'dom'), 0, 0, axis_index_groups=[order], ti...  4.26 us
    ppermute x1, starting transfers between devices, neighbour(): return lax.ppermute(array, 'dom', pairs)  3.88 us
    pallas_call x1, Pallas kernels, fast_shards(): call(functools.partial(upper_body, sections), [SMEM, VMEM, HBM, VMEM, HBM...  3.7 us
    ppermute x6, waiting for transfers between devices, across(): return lax.ppermute(array, 'dom', [(i, i ^ 2 * k) for i in range(domains)])  3.04 us
    all_to_all x1, waiting for transfers between devices, fast_shards(): lax.all_to_all(lower, ('sec', 'dom'), 0, 0, axis_index_groups=[order], ti...  3.02 us
    ppermute x3, waiting for transfers between devices, partner(): return lax.ppermute(array, 'dom', [(i, i ^ 1) for i in range(domains)])  2.33 us
  transfers between devices with their start and end apart: 11, of which 7 were waited for; matrix products, arithmetic and copies ran while one was open for 0% of the time, Pallas kernels for 14%

commit v1 on v0

--- a/solution.py
+++ b/solution.py
@@ -191,45 +191,9 @@
     own_ref[...] = ids[:, 0:LANES]
 
 
-def wall_body(
-    halo, me_ref, ids_ref, mine_ref, theirs_ref, own_ref, near_ref, far_ref, flow_ref, wt_ref, pivots_ref,
-    wall_ref, permuted_ref, ping, pong,
-):
-    me = me_ref[0]
-    odd = me % 2
-    is_odd = odd == 1
-    chips = mine_ref.shape[0]
-    comps, cells, width = flow_ref.shape
-    count, _, block = wt_ref.shape
-    halves = block // width
-    ids_at = halo * (comps + count * halves)
-
-    slot = lax.broadcasted_iota(jnp.int32, (SUB * 3, 2 * chips), 1)
-    chip = (me // 2) ^ (slot % chips)
-    core = odd ^ (slot // chips)
-    block_of = (2 * chip + core).astype(jnp.float32)
-    ids = jnp.concatenate(
-        [own_ref[:, 0:1], near_ref[ids_at : ids_at + SUB, 0:1], far_ref[ids_at : ids_at + SUB, 0:1]],
-        axis=0,
-    )
-    choose = (ids == block_of).astype(jnp.bfloat16)
-    table = jnp.concatenate([mine_ref[...], theirs_ref[...]], axis=0).astype(jnp.bfloat16)
-    picked = jnp.dot(choose, table, preferred_element_type=jnp.float32)
-
-    own = jnp.zeros((cells, LANES), jnp.float32)
-    edge = [jnp.zeros((halo, LANES), jnp.float32) for _ in range(2)]
-    for k in range(count):
-        weights = wt_ref[k].astype(jnp.float32)
-        for q in range(0, block, LANES):
-            own += weights[:, q : q + LANES] * picked[k : k + 1, q : q + LANES]
-            rows = halo * (comps + k * halves + q // width)
-            for e, ref in enumerate((near_ref, far_ref)):
-                edge[e] += (
-                    ref[rows : rows + halo, q % width : q % width + LANES]
-                    * picked[SUB * (e + 1) + k : SUB * (e + 1) + k + 1, q : q + LANES]
-                )
-    own = jnp.sum(own, axis=1, keepdims=True)
-    near, far = [jnp.sum(e, axis=1, keepdims=True) for e in edge]
+def still_body(halo, me_ref, near_ref, far_ref, flow_ref, still_ref, answer_ref, ping, pong):
+    is_odd = me_ref[0] % 2 == 1
+    _, cells, _ = flow_ref.shape
 
     def beside(load):
         group = lane_index((1, LANES)) // GROUP
@@ -242,20 +206,25 @@
     ]
     first = lane_index((1, LANES)) == 2 * GROUP
     parts = [
-        (0, jnp.where(is_odd, near, far), jnp.where(is_odd, at_near, at_far)),
-        (halo, own, beside(lambda c: flow_ref[c])),
-        (halo + cells, jnp.where(is_odd, far, near), jnp.where(is_odd, at_far, at_near)),
+        (0, jnp.where(is_odd, at_near, at_far)),
+        (halo, beside(lambda c: flow_ref[c])),
+        (halo + cells, jnp.where(is_odd, at_far, at_near)),
     ]
-    for at, column, part in parts:
-        rows = column.shape[0]
-        column = jnp.broadcast_to(column, (rows, LANES))
-        wall_ref[at : at + rows, :] = column
-        ping[SUB + at : SUB + at + rows, :] = jnp.where(first, column, part)
-
-    extent = cells + 2 * halo
+    for at, part in parts:
+        ping[SUB + at : SUB + at + part.shape[0], :] = jnp.where(first, 0.0, part)
+
+    unit = SUB + cells + 3 * halo
+    shape = (4 * halo, LANES)
+    row = lax.broadcasted_iota(jnp.int32, shape, 0)
+    ping[unit : unit + 4 * halo, :] = jnp.where((row == 2 * halo) & first, 1.0, 0.0)
+    for ref in (ping, pong):
+        ref[unit + 4 * halo :, :] = jnp.zeros((SUB, LANES), jnp.float32)
+    ping[unit - halo : unit, :] = jnp.zeros((halo, LANES), jnp.float32)
+
+    total = unit + 4 * halo - SUB
     src, dst = ping, pong
-    for index in range(ITERS):
-        at, rows = (SUB, extent) if index < ITERS - 1 else (SUB + halo, cells)
+    for _ in range(ITERS):
+        at, rows = SUB, total
         lane = lane_index((rows, LANES))
         group = lane // GROUP
         height = lane % GROUP
@@ -276,11 +245,66 @@
         cross = jnp.where(group == 0, pltpu.roll(z_slope, LANES - GROUP, 1) + other_y, other_y)
         cross = jnp.where(group == 1, pltpu.roll(z_slope, GROUP, 1), cross)
         value = centre - COURANT * (MACH * z_slope + cross) - damping
-        if index < ITERS - 1:
-            dst[at : at + rows, :] = jnp.where(group == 3, 0.0, value)
+        dst[at : at + rows, :] = jnp.where(group == 3, 0.0, value)
         src, dst = dst, src
-    push = (FACE_AREA * value[:, 0:1]).astype(jnp.bfloat16).astype(jnp.float32)
-    push = jnp.broadcast_to(push, (cells, LANES))
+    still_ref[...] = jnp.broadcast_to(src[SUB + halo : SUB + halo + cells, 0:1], still_ref.shape)
+    answer_ref[...] = jnp.broadcast_to(
+        src[unit + halo : unit + halo + answer_ref.shape[0], 0:1], answer_ref.shape
+    )
+
+
+def wall_body(
+    halo, me_ref, ids_ref, mine_ref, theirs_ref, own_ref, near_ref, far_ref, still_ref, answer_ref,
+    wt_ref, pivots_ref, wall_ref, permuted_ref,
+):
+    me = me_ref[0]
+    odd = me % 2
+    is_odd = odd == 1
+    chips = mine_ref.shape[0]
+    cells, width = still_ref.shape[0], near_ref.shape[1]
+    count, _, block = wt_ref.shape
+    halves = block // width
+    comps = (near_ref.shape[0] - SUB) // halo - count * halves
+    ids_at = halo * (comps + count * halves)
+
+    slot = lax.broadcasted_iota(jnp.int32, (SUB * 3, 2 * chips), 1)
+    chip = (me // 2) ^ (slot % chips)
+    core = odd ^ (slot // chips)
+    block_of = (2 * chip + core).astype(jnp.float32)
+    ids = jnp.concatenate(
+        [own_ref[:, 0:1], near_ref[ids_at : ids_at + SUB, 0:1], far_ref[ids_at : ids_at + SUB, 0:1]],
+        axis=0,
+    )
+    choose = (ids == block_of).astype(jnp.bfloat16)
+    table = jnp.concatenate([mine_ref[...], theirs_ref[...]], axis=0).astype(jnp.bfloat16)
+    picked = jnp.dot(choose, table, preferred_element_type=jnp.float32)
+
+    own = jnp.zeros((cells, LANES), jnp.float32)
+    edge = [jnp.zeros((halo, LANES), jnp.float32) for _ in range(2)]
+    for k in range(count):
+        weights = wt_ref[k].astype(jnp.float32)
+        for q in range(0, block, LANES):
+            own += weights[:, q : q + LANES] * picked[k : k + 1, q : q + LANES]
+            rows = halo * (comps + k * halves + q // width)
+            for e, ref in enumerate((near_ref, far_ref)):
+                edge[e] += (
+                    ref[rows : rows + halo, q % width : q % width + LANES]
+                    * picked[SUB * (e + 1) + k : SUB * (e + 1) + k + 1, q : q + LANES]
+                )
+    own = jnp.sum(own, axis=1, keepdims=True)
+    near, far = [jnp.sum(e, axis=1, keepdims=True) for e in edge]
+
+    for at, column in (
+        (0, jnp.where(is_odd, near, far)),
+        (halo, own),
+        (halo + cells, jnp.where(is_odd, far, near)),
+    ):
+        rows = column.shape[0]
+        wall_ref[at : at + rows, :] = jnp.broadcast_to(column, (rows, LANES))
+    value = still_ref[...]
+    for m in range(2 * halo + 1):
+        value = value + answer_ref[m : m + 1, :] * wall_ref[2 * halo - m : 2 * halo - m + cells, :]
+    push = (FACE_AREA * value).astype(jnp.bfloat16).astype(jnp.float32)
 
     pivot = pivots_ref[...]
     row = jnp.right_shift(pivot, LANES.bit_length() - 1)
@@ -492,15 +516,23 @@
     theirs = partner(mine)
 
     extent = cells + 2 * halo
+    still, answer = call(
+        functools.partial(still_body, halo),
+        [SMEM] + [VMEM] * 3,
+        (f32(cells, LANES), f32(3 * halo, LANES)),
+        [pltpu.VMEM((cells + 7 * halo + 2 * SUB, LANES), jnp.float32)] * 2,
+        (COVER, 40_000_000),
+        4 << 20,
+    )(me, near, far, field)
     pivot_rows = pivots.reshape(-1, LANES)
     wall, permuted = call(
         functools.partial(wall_body, halo),
-        [SMEM, SMEM] + [VMEM] * 8,
+        [SMEM, SMEM] + [VMEM] * 9,
         (f32(extent, LANES), f32(*pivot_rows.shape)),
-        [pltpu.VMEM((extent + 2 * SUB, LANES), jnp.float32)] * 2,
+        [],
         (COVER, 40_000_000),
-        8 << 20,
-    )(me, ids, mine, theirs, own, near, far, field, weights, pivot_rows)
+        4 << 20,
+    )(me, ids, mine, theirs, own, near, far, still, answer, weights, pivot_rows)
 
     pair = permuted + partner(permuted)
     pieces = [pair] + [across(pair, k) for k in range(chips - 1, 0, -1)]

time: 42.2 us -> 42.5 us (level)
    ppermute x3, waiting for transfers between devices: 2.33 us -> 1.18 us  [partner(): return lax.ppermute(array, 'dom', [(i, i ^ 1) for i in range(domains)])]
    ppermute x1, waiting for transfers between devices: 1.93 us -> 3.05 us  [neighbour(): return lax.ppermute(array, 'dom', pairs)]
    pallas_call x1 -> x2, Pallas kernels: 1.73 us -> 2.09 us  [the longest x1 1.2 us: fast_shards(): call(functools.partial(wall_body, halo), [SMEM, SMEM] + [VMEM] * 9, (f32(...]
  transfers between devices with their start and end apart: 11 -> 11, of which waited for: 7 -> 6; matrix products, arithmetic and copies ran while one was open for 0% -> 0% of each run, Pallas kernels for 14% -> 15%
where the time goes in v1:
time: 42.5 us; the launch traced here: 42.2 us
  starting transfers between devices  18.5 us (44%)
  Pallas kernels  12.6 us (30%)
  waiting for transfers between devices  10.3 us (24%)
  between operations  0.78 us (2%)
    ppermute x6, starting transfers between devices, across(): return lax.ppermute(array, 'dom', [(i, i ^ 2 * k) for i in range(domains)])  10.2 us
    pallas_call x1, Pallas kernels, fast_shards(): call(functools.partial(flow_body, halo), [SMEM, VMEM, VMEM, HBM, VMEM, HB...  4.56 us
    all_to_all x1, starting transfers between devices, fast_shards(): lax.all_to_all(lower, ('sec', 'dom'), 0, 0, axis_index_groups=[order], ti...  4.26 us
    ppermute x1, starting transfers between devices, neighbour(): return lax.ppermute(array, 'dom', pairs)  3.9 us
    pallas_call x1, Pallas kernels, fast_shards(): call(functools.partial(upper_body, sections), [SMEM, VMEM, HBM, VMEM, HBM...  3.7 us
    ppermute x1, waiting for transfers between devices, neighbour(): return lax.ppermute(array, 'dom', pairs)  3.05 us
    ppermute x6, waiting for transfers between devices, across(): return lax.ppermute(array, 'dom', [(i, i ^ 2 * k) for i in range(domains)])  3.04 us
    all_to_all x1, waiting for transfers between devices, fast_shards(): lax.all_to_all(lower, ('sec', 'dom'), 0, 0, axis_index_groups=[order], ti...  3.02 us
  transfers between devices with their start and end apart: 11, of which 6 were waited for; matrix products, arithmetic and copies ran while one was open for 0% of the time, Pallas kernels for 15%

profile of v1, /device:TPU:0, one launch (start us, length us, event | category | flops | bytes accessed | tf_op | source)
XLA Modules:
  0.0 42.2 jit_solution(17130044326102810208)
XLA Ops:
  0.6 5.1 %collective-permute-start.4 = (f32[1,512]{1,0:T(1,128)}, f32[1,512]{1,0:T(1,128)S(1)}, u32[]{:S(2)}, u32[]{:S(2)}) collective-permute-start(f32[1,512]{1,0:T(1,128)} %bitcast.20), channel_id=1, source_target_pairs={{0,6},{1,7},{2,4},{3,5},{4,2},{5,3},{6,0},{7,1},{8,14},{9,15},{10,... | collective-permute-start | bytes 6152 | tf_op jit(solution)/shard_map/ppermute | solution.py:486
  5.8 1.0 %shard_map.86 = (f32[104,256]{1,0:T(8,128)S(1)}, f32[104,256]{1,0:T(8,128)S(1)}, f32[8,128]{1,0:T(8,128)S(1)}, f32[1,512]{1,0:T(1,128)S(1)}) custom-call(s32[1]{0:T(128)} %bitcast.me_ref, s32[4]{0:T(128)} %bitcast.18, f32[1,512]{1,0:T(1,128)} %bitcast.21, f32[4,64,256]{2,1,0:T(8,128)} %bitcast.14, bf16[4,64,512]{2,1,0:T(8,128)(2,1)} %bitcast.12), custom_call_target="tpu_custom_call" | custom-call | flops 20000000000 | bytes 400000 | tf_op jit(solution)/shard_map/pallas_call | solution.py:497
  6.8 0.1 collective-permute-start.3
  6.9 0.6 %collective-permute-start.2 = (f32[1,512]{1,0:T(1,128)S(1)}, f32[1,512]{1,0:T(1,128)S(1)}, u32[]{:S(2)}, u32[]{:S(2)}) collective-permute-start(f32[1,512]{1,0:T(1,128)S(1)} %get-tuple-element.14), channel_id=1, source_target_pairs={{0,2},{1,3},{2,0},{3,1},{4,6},{5,7},{6,4},{7,5},{8,10},{9,11},{10,... | collective-permute-start | bytes 6152 | tf_op jit(solution)/shard_map/ppermute | solution.py:486
  7.5 0.0 collective-permute-start
  7.5 3.9 %collective-permute-start.1 = (f32[104,256]{1,0:T(8,128)S(1)}, f32[104,256]{1,0:T(8,128)S(1)}, u32[]{:S(2)}, u32[]{:S(2)}) collective-permute-start(f32[104,256]{1,0:T(8,128)S(1)} %get-tuple-element.13), channel_id=1, source_target_pairs={{0,7},{1,2},{2,1},{3,4},{4,3},{5,6},{6,5},{7,0},{8,15},{9,10},{10,... | collective-permute-start | bytes 319496 | tf_op jit(solution)/shard_map/ppermute | solution.py:493
  11.4 0.0 collective-permute-done.4
  11.4 0.1 collective-permute-done.3
  11.5 0.0 collective-permute-done.2
  11.5 0.0 copy-start
  11.5 0.0 copy-start.2
  11.5 0.0 copy-start.3
  11.5 0.1 collective-permute-start.5
  11.6 0.0 collective-permute-done.near_ref
  11.6 3.0 %collective-permute-done.1.far_ref = f32[104,256]{1,0:T(8,128)S(1)} collective-permute-done((f32[104,256]{1,0:T(8,128)S(1)}, f32[104,256]{1,0:T(8,128)S(1)}, u32[]{:S(2)}, u32[]{:S(2)}) %collective-permute-start.1) | collective-permute-done | bytes 106528 | tf_op jit(solution)/shard_map/ppermute | solution.py:493
  14.7 0.9 %shard_map.87 = (f32[64,128]{1,0:T(8,128)S(1)}, f32[24,128]{1,0:T(8,128)S(1)}) custom-call(s32[1]{0:T(128)} %bitcast.me_ref, f32[104,256]{1,0:T(8,128)S(1)} %collective-permute-done.near_ref, f32[104,256]{1,0:T(8,128)S(1)} %collective-permute-done.1.far_ref, f32[4,64,256]{2,1,0:T(8,128)S(1)} %bitcast.16), custom_call_target="tpu_custom_call" | custom-call | flops 20000000000 | bytes 40000000 | tf_op jit(solution)/shard_map/pallas_call | solution.py:519
  15.5 0.0 collective-permute-done.5.theirs_ref
  15.6 0.0 slice-start.1
  15.6 1.2 %shard_map.88 = (f32[80,128]{1,0:T(8,128)S(1)}, f32[32,128]{1,0:T(8,128)S(1)}) custom-call(s32[1]{0:T(128)} %bitcast.me_ref, s32[4]{0:T(128)S(1)} %bitcast.19, f32[4,512]{1,0:T(4,128)S(1)} %pad_maximum_fusion.mine_ref, f32[4,512]{1,0:T(4,128)S(1)} %collective-permute-done.5.theirs_ref, f32[8,128]{1,0:T(8,128)S(1)} %get-tuple-element.15.own_ref, ...), custom_call_target="tpu_custom_call" | custom-call | flops 20000000000 | bytes 40000000 | tf_op jit(solution)/shard_map/pallas_call | solution.py:528
  16.8 0.1 collective-permute-start.6
  16.9 1.2 %collective-permute-done.6 = f32[32,128]{1,0:T(8,128)S(1)} collective-permute-done((f32[32,128]{1,0:T(8,128)S(1)}, f32[32,128]{1,0:T(8,128)S(1)}, u32[]{:S(2)}, u32[]{:S(2)}) %collective-permute-start.6) | collective-permute-done | bytes 16416 | tf_op jit(solution)/shard_map/ppermute | solution.py:489
  18.1 2.7 %collective-permute-start.7 = (f32[32,128]{1,0:T(8,128)S(1)}, f32[32,128]{1,0:T(8,128)S(1)}, u32[]{:S(2)}, u32[]{:S(2)}) collective-permute-start(f32[32,128]{1,0:T(8,128)S(1)} %add.3.refs_0_), channel_id=1, source_target_pairs={{0,6},{1,7},{2,4},{3,5},{4,2},{5,3},{6,0},{7,1},{8,14},{9,15},{10,... | collective-permute-start | bytes 49160 | tf_op jit(solution)/shard_map/ppermute | solution.py:486
  20.8 0.0 collective-permute-start.8
  20.8 1.7 %collective-permute-start.9 = (f32[32,128]{1,0:T(8,128)S(1)}, f32[32,128]{1,0:T(8,128)S(1)}, u32[]{:S(2)}, u32[]{:S(2)}) collective-permute-start(f32[32,128]{1,0:T(8,128)S(1)} %add.3.refs_0_), channel_id=1, source_target_pairs={{0,2},{1,3},{2,0},{3,1},{4,6},{5,7},{6,4},{7,5},{8,10},{9,11},{10,... | collective-permute-start | bytes 49160 | tf_op jit(solution)/shard_map/ppermute | solution.py:486
  22.4 1.2 %collective-permute-done.7.refs_1_ = f32[32,128]{1,0:T(8,128)S(1)} collective-permute-done((f32[32,128]{1,0:T(8,128)S(1)}, f32[32,128]{1,0:T(8,128)S(1)}, u32[]{:S(2)}, u32[]{:S(2)}) %collective-permute-start.7) | collective-permute-done | bytes 16416 | tf_op jit(solution)/shard_map/ppermute | solution.py:486
  23.6 1.8 %collective-permute-done.8.refs_2_ = f32[32,128]{1,0:T(8,128)S(1)} collective-permute-done((f32[32,128]{1,0:T(8,128)S(1)}, f32[32,128]{1,0:T(8,128)S(1)}, u32[]{:S(2)}, u32[]{:S(2)}) %collective-permute-start.8) | collective-permute-done | bytes 16416 | tf_op jit(solution)/shard_map/ppermute | solution.py:486
  25.4 0.0 collective-permute-done.9.refs_3_
  25.4 1.3 %shard_map.90 = f32[32,1,512]{2,1,0:T(1,128)} custom-call(f32[32,128]{1,0:T(8,128)S(1)} %add.3.refs_0_, f32[32,128]{1,0:T(8,128)S(1)} %collective-permute-done.7.refs_1_, f32[32,128]{1,0:T(8,128)S(1)} %collective-permute-done.8.refs_2_, f32[32,128]{1,0:T(8,128)S(1)} %collective-permute-done.9.refs_3_, f32[512,4096]{1,0:T(8,128)S(1)} %bitcast.11), custom_call_target="tpu_custom_call" | custom-call | flops 20000000000 | bytes 1000000 | tf_op jit(solution)/shard_map/pallas_call | solution.py:550
  26.7 4.3 %all-to-all-start = ((f32[32,1,512]{2,1,0:T(1,128)}), f32[32,1,512]{2,1,0:T(1,128)S(1)}, u32[]{:S(2)}, u32[]{:S(2)}) async-start(f32[32,1,512]{2,1,0:T(1,128)} %shard_map.90), calls=%async_computation | async-start | bytes 131072 | tf_op jit(solution)/shard_map/all_to_all | solution.py:559
  31.0 4.6 %shard_map.89 = (f32[4,64,256]{2,1,0:T(8,128)}, f32[512,1024]{1,0:T(8,128)S(1)}) custom-call(s32[1]{0:T(128)} %bitcast.me_ref, f32[104,256]{1,0:T(8,128)S(1)} %collective-permute-done.near_ref, f32[104,256]{1,0:T(8,128)S(1)} %collective-permute-done.1.far_ref, f32[4,64,256]{2,1,0:T(8,128)} %bitcast.15, f32[80,128]{1,0:T(8,128)S(1)} %get-tuple-element.18.wall_ref, ...), custom_call_target="tpu_custom_call" | custom-call | flops 20000000000 | bytes 4000000 | tf_op jit(solution)/shard_map/pallas_call | solution.py:540
  35.5 3.0 %all-to-all-done.parts_ref = f32[32,1,512]{2,1,0:T(1,128)S(1)} async-done(((f32[32,1,512]{2,1,0:T(1,128)}), f32[32,1,512]{2,1,0:T(1,128)S(1)}, u32[]{:S(2)}, u32[]{:S(2)}) %all-to-all-start) | async-done | bytes 65568 | tf_op jit(solution)/shard_map/all_to_all | solution.py:559
  38.5 3.7 %shard_map.91 = f32[1,512]{1,0:T(1,128)} custom-call(s32[1]{0:T(128)} %bitcast.me_ref, f32[32,1,512]{2,1,0:T(1,128)S(1)} %all-to-all-done.parts_ref, f32[1,512]{1,0:T(1,128)} %bitcast.22, f32[512,1024]{1,0:T(8,128)S(1)} %get-tuple-element.21.tail_ref, f32[512,4096]{1,0:T(8,128)} %front_hbm.3), custom_call_target="tpu_custom_call" | custom-call | flops 20000000000 | bytes 1000000 | tf_op jit(solution)/shard_map/pallas_call | solution.py:562
  (11 shorter events, 0.0 us)
Async XLA Ops:
  0.6 10.7 %collective-permute-start.4 = (f32[1,512]{1,0:T(1,128)}, f32[1,512]{1,0:T(1,128)S(1)}, u32[]{:S(2)}, u32[]{:S(2)}) collective-permute-start(f32[1,512]{1,0:T(1,128)} %bitcast.20), channel_id=1, source_target_pairs={{0,6},{1,7},{2,4},{3,5},{4,2},{5,3},{6,0},{7,1},{8,14},{9,15},{10,... | collective-permute-start | bytes 6152 | tf_op jit(solution)/shard_map/ppermute | solution.py:486
  5.8 8.9 %copy-start.1 = (f32[1,4,64,256]{3,2,1,0:T(8,128)S(1)}, f32[1,4,64,256]{3,2,1,0:T(8,128)}, u32[]{:S(2)}) copy-start(f32[1,4,64,256]{3,2,1,0:T(8,128)} %param.10) | copy-start | bytes 786436
  6.8 4.6 %collective-permute-start.3 = (f32[1,512]{1,0:T(1,128)S(1)}, f32[1,512]{1,0:T(1,128)S(1)}, u32[]{:S(2)}, u32[]{:S(2)}) collective-permute-start(f32[1,512]{1,0:T(1,128)S(1)} %get-tuple-element.14), channel_id=1, source_target_pairs={{0,4},{1,5},{2,6},{3,7},{4,0},{5,1},{6,2},{7,3},{8,12},{9,13},{10,... | collective-permute-start | bytes 6152 | tf_op jit(solution)/shard_map/ppermute | solution.py:486
  6.9 4.6 %collective-permute-start.2 = (f32[1,512]{1,0:T(1,128)S(1)}, f32[1,512]{1,0:T(1,128)S(1)}, u32[]{:S(2)}, u32[]{:S(2)}) collective-permute-start(f32[1,512]{1,0:T(1,128)S(1)} %get-tuple-element.14), channel_id=1, source_target_pairs={{0,2},{1,3},{2,0},{3,1},{4,6},{5,7},{6,4},{7,5},{8,10},{9,11},{10,... | collective-permute-start | bytes 6152 | tf_op jit(solution)/shard_map/ppermute | solution.py:486
  7.5 4.1 %collective-permute-start = (f32[104,256]{1,0:T(8,128)S(1)}, f32[104,256]{1,0:T(8,128)S(1)}, u32[]{:S(2)}, u32[]{:S(2)}) collective-permute-start(f32[104,256]{1,0:T(8,128)S(1)} %get-tuple-element.12), channel_id=1, source_target_pairs={{0,1},{1,0},{2,3},{3,2},{4,5},{5,4},{6,7},{7,6},{8,9},{9,8},{10,11... | collective-permute-start | bytes 319496 | tf_op jit(solution)/shard_map/ppermute | solution.py:489
  7.5 7.2 %collective-permute-start.1 = (f32[104,256]{1,0:T(8,128)S(1)}, f32[104,256]{1,0:T(8,128)S(1)}, u32[]{:S(2)}, u32[]{:S(2)}) collective-permute-start(f32[104,256]{1,0:T(8,128)S(1)} %get-tuple-element.13), channel_id=1, source_target_pairs={{0,7},{1,2},{2,1},{3,4},{4,3},{5,6},{6,5},{7,0},{8,15},{9,10},{10,... | collective-permute-start | bytes 319496 | tf_op jit(solution)/shard_map/ppermute | solution.py:493
  11.5 4.1 %copy-start = (bf16[1,1,4,512,64]{3,4,2,1,0:T(8,128)(2,1)S(1)}, bf16[1,1,4,512,64]{3,4,2,1,0:T(8,128)(2,1)}, u32[]{:S(2)}) copy-start(bf16[1,1,4,512,64]{3,4,2,1,0:T(8,128)(2,1)} %param.9) | copy-start | bytes 786436
  11.5 4.1 %copy-start.2 = (s32[4096]{0:T(1024)S(1)}, s32[4096]{0:T(1024)}, u32[]{:S(2)}) copy-start(s32[4096]{0:T(1024)} %param.11) | copy-start | bytes 49156
  11.5 4.1 %copy-start.3 = (s32[1,1,4]{2,1,0:T(1,128)S(1)}, s32[1,1,4]{2,1,0:T(1,128)}, u32[]{:S(2)}) copy-start(s32[1,1,4]{2,1,0:T(1,128)} %param.8) | copy-start | bytes 52
  11.5 4.0 %collective-permute-start.5 = (f32[4,512]{1,0:T(4,128)S(1)}, f32[4,512]{1,0:T(4,128)S(1)}, u32[]{:S(2)}, u32[]{:S(2)}) collective-permute-start(f32[4,512]{1,0:T(4,128)S(1)} %pad_maximum_fusion.mine_ref), channel_id=1, source_target_pairs={{0,1},{1,0},{2,3},{3,2},{4,5},{5,4},{6,7},{7,6},{8,9},{9,8},{10,11... | collective-permute-start | bytes 24584 | tf_op jit(solution)/shard_map/ppermute | solution.py:489
  14.7 10.7 %slice-start = ((s8[8388608]{0:T(1024)(128)(4,1)}), s8[4194304]{0:T(1024)(128)(4,1)S(1)}, s32[]{:S(2)}) async-start(s8[8388608]{0:T(1024)(128)(4,1)} %bitcast.10), calls=%async_computation.1 | async-start | bytes 8388608
  15.6 9.8 %slice-start.1 = ((s8[8388608]{0:T(1024)(128)(4,1)}), s8[4194304]{0:T(1024)(128)(4,1)S(1)}, s32[]{:S(2)}) async-start(s8[8388608]{0:T(1024)(128)(4,1)} %bitcast.10), calls=%async_computation.2 | async-start | bytes 8388608
  16.8 1.2 %collective-permute-start.6 = (f32[32,128]{1,0:T(8,128)S(1)}, f32[32,128]{1,0:T(8,128)S(1)}, u32[]{:S(2)}, u32[]{:S(2)}) collective-permute-start(f32[32,128]{1,0:T(8,128)S(1)} %get-tuple-element.20), channel_id=1, source_target_pairs={{0,1},{1,0},{2,3},{3,2},{4,5},{5,4},{6,7},{7,6},{8,9},{9,8},{10,11... | collective-permute-start | bytes 49160 | tf_op jit(solution)/shard_map/ppermute | solution.py:489
  18.1 5.6 %collective-permute-start.7 = (f32[32,128]{1,0:T(8,128)S(1)}, f32[32,128]{1,0:T(8,128)S(1)}, u32[]{:S(2)}, u32[]{:S(2)}) collective-permute-start(f32[32,128]{1,0:T(8,128)S(1)} %add.3.refs_0_), channel_id=1, source_target_pairs={{0,6},{1,7},{2,4},{3,5},{4,2},{5,3},{6,0},{7,1},{8,14},{9,15},{10,... | collective-permute-start | bytes 49160 | tf_op jit(solution)/shard_map/ppermute | solution.py:486
  20.8 4.6 %collective-permute-start.8 = (f32[32,128]{1,0:T(8,128)S(1)}, f32[32,128]{1,0:T(8,128)S(1)}, u32[]{:S(2)}, u32[]{:S(2)}) collective-permute-start(f32[32,128]{1,0:T(8,128)S(1)} %add.3.refs_0_), channel_id=1, source_target_pairs={{0,4},{1,5},{2,6},{3,7},{4,0},{5,1},{6,2},{7,3},{8,12},{9,13},{10,... | collective-permute-start | bytes 49160 | tf_op jit(solution)/shard_map/ppermute | solution.py:486
  20.8 4.6 %collective-permute-start.9 = (f32[32,128]{1,0:T(8,128)S(1)}, f32[32,128]{1,0:T(8,128)S(1)}, u32[]{:S(2)}, u32[]{:S(2)}) collective-permute-start(f32[32,128]{1,0:T(8,128)S(1)} %add.3.refs_0_), channel_id=1, source_target_pairs={{0,2},{1,3},{2,0},{3,1},{4,6},{5,7},{6,4},{7,5},{8,10},{9,11},{10,... | collective-permute-start | bytes 49160 | tf_op jit(solution)/shard_map/ppermute | solution.py:486
  26.7 11.9 %all-to-all-start = ((f32[32,1,512]{2,1,0:T(1,128)}), f32[32,1,512]{2,1,0:T(1,128)S(1)}, u32[]{:S(2)}, u32[]{:S(2)}) async-start(f32[32,1,512]{2,1,0:T(1,128)} %shard_map.90), calls=%async_computation | async-start | bytes 131072 | tf_op jit(solution)/shard_map/all_to_all | solution.py:559
